TPU v7x, 256 devices: a whole 4x4x8 slice. The times are simulated.
256 devices in a mesh: copy: 2 (over y_hi), dp: 8 (over x, core), fsdp: 16 (over y_lo, z).
Axes of the slice: x: 4, y: 4 (y_hi: 2, y_lo: 2; y = y_hi * 2 + y_lo), z: 8, core: 2. Of those that a mesh axis runs over, the one named last changes fastest.
Arguments:
- queries: bfloat16 [2, 128, 256, 2560], P('copy', ('dp', 'fsdp')), may hold values from -25 to 25
- keys: bfloat16 [2, 128, 256, 2560], P('copy', ('dp', 'fsdp')), may hold values from -25 to 25
- values: bfloat16 [2, 128, 256, 2560], P('copy', ('dp', 'fsdp')), may hold values from -6 to 6
- residual: bfloat16 [2, 128, 256, 2560], P('copy', ('dp', 'fsdp')), may hold values from -6 to 6
- event_ids: int32 [128, 256], P(('dp', 'fsdp')), may hold values from 0 to 1023
- lengths: int32 [128], replicated, may hold values from 8 to 256, as said below
- type_weight: float32 [1024], replicated, may hold values from 0.25 to 4
- w_out: bfloat16 [2, 2560, 2560], P('copy', 'fsdp'), may hold values from -0.125 to 0.125
- gain: float32 [2, 2560], P('copy'), may hold values from 0.5 to 1.5
Outputs:
- loss: float32 [2, 128], P('copy', ('dp', 'fsdp'))
- d_queries: bfloat16 [2, 128, 256, 2560], P('copy', ('dp', 'fsdp'))
- d_keys: bfloat16 [2, 128, 256, 2560], P('copy', ('dp', 'fsdp'))
- d_values: bfloat16 [2, 128, 256, 2560], P('copy', ('dp', 'fsdp'))
- d_wo: float32 [2, 2560, 2560], P('copy', 'fsdp')
Inputs may be any that keep to these rules, and one draw needn't show every extreme that they name: `lengths`: every history has at least 8 valid events and some history has all 256.
All inputs are finite; a program needn't handle non-finite values.
Results may differ from a plain program's by a relative error of at most 0.02.
Values may be sent and summed in bfloat16 or wider, within the bound.
A program may use at most 128 MiB of HBM per device.

v0:
```python
import jax
import jax.numpy as jnp
from jax import lax
from jax.sharding import PartitionSpec as P

DH = 128


def partner_2(value, axis, bit):
    return lax.ppermute(value, axis, [(i, i ^ 1 << bit) for i in range(lax.axis_size(axis))])


def body(queries, keys, values, residual, event_ids, lengths, type_weight, w_out, gain):
    seq = queries.shape[2]
    heads_width = queries.shape[3]
    width = residual.shape[3]
    head_size = DH
    heads = heads_width // head_size
    own = lax.axis_index(("dp", "fsdp"))
    length = lengths[own]
    count = jnp.sum(lengths).astype(jnp.float32)
    my_gain = gain[0]
    full_weight = lax.all_gather(w_out[0], "fsdp", axis=0, tiled=True)
    arrange = lambda matrix: matrix
    restore = lambda matrix: matrix
    query_heads = queries[0, 0].reshape(seq, heads, head_size)
    key_heads = keys[0, 0].reshape(seq, heads, head_size)
    value_heads = values[0, 0].reshape(seq, heads, head_size)
    scale = jnp.sqrt(jnp.float32(head_size))
    scores = (
        jnp.einsum("qhd,khd->hqk", query_heads, key_heads, preferred_element_type=jnp.float32)
        / scale
    )
    rows = jnp.arange(seq, dtype=jnp.int32)[:, None]
    cols = jnp.arange(seq, dtype=jnp.int32)[None, :]
    valid = (cols <= rows) & (cols < length)
    scores = jnp.where(valid[None], scores, jnp.float32(-1e30))
    probs = jax.nn.softmax(scores, axis=-1)
    probs_b = probs.astype(jnp.bfloat16)
    attn = (
        jnp.einsum("hqk,khd->qhd", probs_b, value_heads, preferred_element_type=jnp.float32)
        .reshape(seq, heads_width)
        .astype(jnp.bfloat16)
    )
    hidden = residual[0, 0].astype(jnp.float32) + jnp.dot(
        arrange(attn), full_weight, preferred_element_type=jnp.float32
    )
    inv = lax.rsqrt(jnp.mean(hidden * hidden, axis=-1, keepdims=True) + 1e-06)
    normed = hidden * inv
    feat = normed * my_gain[None, :]
    partner = partner_2(feat.astype(jnp.bfloat16), "copy", 0)
    type_count = type_weight.shape[0]
    matches = event_ids[0][:, None] == jnp.arange(type_count, dtype=jnp.int32)[None, :]
    looked_up = jnp.sum(jnp.where(matches, type_weight[None, :], jnp.float32(0.0)), axis=-1)
    live = jnp.arange(seq, dtype=jnp.int32) < length
    tok_w = jnp.where(live, looked_up, jnp.float32(0.0))
    diff = feat - partner.astype(jnp.float32)
    loss = jnp.sum(tok_w * jnp.sum(diff * diff, axis=-1)) / (width * count)
    dfeat = 2.0 * tok_w[:, None] * diff / (width * count)
    scaled = dfeat * my_gain[None, :]
    d_hidden = (inv * (scaled - normed * jnp.mean(normed * scaled, axis=-1, keepdims=True))).astype(
        jnp.bfloat16
    )
    partial_term = jnp.dot(attn.T, d_hidden, preferred_element_type=jnp.float32).astype(
        jnp.bfloat16
    )
    row_sum = lax.psum_scatter(partial_term, "fsdp", scatter_dimension=0, tiled=True).astype(
        jnp.float32
    )
    d_wo = lax.psum(row_sum.astype(jnp.bfloat16), "dp").astype(jnp.float32)
    d_attn_arranged = lax.dot_general(
        d_hidden, full_weight, (((1,), (1,)), ((), ())), preferred_element_type=jnp.float32
    )
    d_attn = restore(d_attn_arranged).astype(jnp.bfloat16)
    d_heads = d_attn.reshape(seq, heads, head_size)
    d_values = (
        jnp.einsum("hqk,qhd->khd", probs_b, d_heads, preferred_element_type=jnp.float32)
        .reshape(seq, heads_width)
        .astype(jnp.bfloat16)
    )
    dprob = jnp.einsum("qhd,khd->hqk", d_heads, value_heads, preferred_element_type=jnp.float32)
    delta = jnp.sum(dprob * probs, axis=-1, keepdims=True)
    ds = (probs * (dprob - delta) / scale).astype(jnp.bfloat16)
    d_queries = (
        jnp.einsum("hqk,khd->qhd", ds, key_heads, preferred_element_type=jnp.float32)
        .reshape(seq, heads_width)
        .astype(jnp.bfloat16)
    )
    d_keys = (
        jnp.einsum("hqk,qhd->khd", ds, query_heads, preferred_element_type=jnp.float32)
        .reshape(seq, heads_width)
        .astype(jnp.bfloat16)
    )
    return (
        loss.reshape(1, 1),
        d_queries[None, None],
        d_keys[None, None],
        d_values[None, None],
        d_wo[None],
    )


def solution(mesh):
    in_specs = (
        P("copy", ("dp", "fsdp"), None, None),
        P("copy", ("dp", "fsdp"), None, None),
        P("copy", ("dp", "fsdp"), None, None),
        P("copy", ("dp", "fsdp"), None, None),
        P(("dp", "fsdp"), None),
        P(),
        P(),
        P("copy", "fsdp", None),
        P("copy", None),
    )
    out_specs = (
        P("copy", ("dp", "fsdp")),
        P("copy", ("dp", "fsdp"), None, None),
        P("copy", ("dp", "fsdp"), None, None),
        P("copy", ("dp", "fsdp"), None, None),
        P("copy", "fsdp", None),
    )
    return jax.shard_map(body, mesh=mesh, in_specs=in_specs, out_specs=out_specs, check_vma=False)
```

profile of v0, /device:TPU:8, one launch (start us, length us, event | category | flops | bytes accessed | tf_op | source)
XLA Modules:
  0.0 438.8 jit_solution(15980191786920070180)
XLA Ops:
  7.2 0.0 copy-start.3
  7.2 0.0 all-gather.3.cloned.1.call-start
  7.2 0.7 all-gather.3.cloned.1.call-update
  7.9 0.0 reduce-scatter.2.cloned.1.call-start
  8.0 1.6 copy.48
  9.6 0.0 copy-start
  9.6 0.0 copy-done.3
  9.6 0.0 copy-start.9
  9.6 0.0 copy-start.6
  9.6 1.4 copy.44
  11.1 0.0 copy-start.4
  11.1 2.5 copy.45
  13.6 0.0 copy-done.9
  13.6 0.6 dynamic_slice.3
  14.2 0.0 copy-done.6
  14.2 0.7 iota_compare_fusion.2
  14.9 0.1 fusion.35
  15.0 0.0 copy-done.4
  15.0 5.6 %fusion.44 = (f32[20,256]{1,0:T(8,128)S(1)}, f32[20,256,256]{1,2,0:T(8,128)}) fusion(pred[256,256]{0,1:T(8,128)(4,1)S(1)} %fusion.35, bf16[256,20,128]{0,2,1:T(8,128)(2,1)S(1)} %bitcast.52, bf16[256,20,128]{0,2,1:T(8,128)(2,1)} %bitcast.54), kind=kOutput, calls=%fused_computation.52 | convolution fusion | flops 340787456 | bytes 7950336 | tf_op jit(solution)/shard_map/sub | solution.py:38
  20.6 0.0 copy-done
  20.6 4.1 convolution_convert_fusion.1
  24.7 135.4 %all-gather.3.cloned.1.call-done = bf16[1,2560,2560]{2,1,0:T(8,128)(2,1)} async-done(((bf16[1,160,2560]{2,1,0:T(8,128)(2,1)}), bf16[1,2560,2560]{2,1,0:T(8,128)(2,1)}) %all-gather.3.cloned.1.call-update) | async-done | bytes 13107216 | tf_op jit(solution)/shard_map/all_gather | solution.py:23
  160.1 9.2 %multiply_reduce_fusion.3 = (f32[256]{0:T(256)S(1)}, f32[256,2560]{1,0:T(8,128)S(1)}) fusion(bf16[256,2560]{0,1:T(8,128)(2,1)} %bitcast.50, bf16[1,2560,2560]{2,1,0:T(8,128)(2,1)} %all-gather.3.cloned.1.call-done, bf16[1,1,256,2560]{3,2,1,0:T(8,128)(2,1)} %param.12), kind=kOutput, calls=%fused_computation.22 | convolution fusion | flops 3358064384 | bytes 18351104 | tf_op jit(solution)/shard_map/dot_general | solution.py:45
  169.2 0.0 copy-start.7
  169.3 0.0 copy-start.8
  169.3 1.3 multiply_convert_fusion.2
  170.6 2.4 collective-permute-start
  173.0 0.7 reduce_sum.77
  174.3 0.0 copy-start.2
  174.3 0.0 copy-done.7
  174.3 0.0 copy-done.8
  174.3 0.2 select_reduce_fusion
  174.6 0.8 select_multiply_fusion
  175.4 27.4 %collective-permute-done = bf16[256,2560]{1,0:T(8,128)(2,1)} collective-permute-done((bf16[256,2560]{1,0:T(8,128)(2,1)}, bf16[256,2560]{1,0:T(8,128)(2,1)}, u32[]{:S(2)}, u32[]{:S(2)}) %collective-permute-start) | collective-permute-done | bytes 1310752 | tf_op jit(solution)/shard_map/ppermute | solution.py:10
  202.8 2.4 multiply_reduce_fusion.1
  205.3 0.0 copy-done.2
  205.3 8.6 %convolution_convert_fusion = bf16[2560,2560]{1,0:T(8,128)(2,1)} fusion(bf16[256,2560]{0,1:T(8,128)(2,1)S(1)} %bitcast.51, f32[256,2560]{1,0:T(8,128)S(1)} %get-tuple-element.25, bf16[256,2560]{1,0:T(8,128)(2,1)} %collective-permute-done, f32[256]{0:T(256)S(1)} %broadcast_multiply_fusion, f32[]{:T(128)S(6)} %mul.91, f32[256]{0:T(256)S(1)} %select_multiply_fusion, ...), kind=kOutput, calls=%fused_computation.2 | convolution fusion | flops 3369205760 | bytes 18363396 | tf_op jit(solution)/shard_map/dot_general | solution.py:64
  213.9 0.0 reduce-scatter.2.cloned.1.call-update
  213.9 0.2 all-reduce.2.cloned.1.call-start
  214.1 1.2 multiply_reduce_fusion.4
  216.0 10.0 %fusion.11 = bf16[256,2560]{1,0:T(8,128)(2,1)} fusion(bf16[1,2560,2560]{2,1,0:T(8,128)(2,1)} %all-gather.3.cloned.1.call-done, f32[256,2560]{1,0:T(8,128)S(1)} %get-tuple-element.25, bf16[256,2560]{1,0:T(8,128)(2,1)} %collective-permute-done, f32[256]{0:T(256)S(1)} %broadcast_multiply_fusion, f32[]{:T(128)S(6)} %mul.91, f32[256]{0:T(256)S(1)} %select_multiply_fusion, ...), kind=kOutput, calls=%fused_computation.14 | convolution fusion | flops 3363307520 | bytes 18363396 | tf_op jit(solution)/shard_map/dot_general | solution.py:71
  226.1 0.0 copy-start.1
  226.1 1.7 copy.50
  227.8 0.0 copy-done.1
  227.8 3.2 fusion.45
  231.0 10.4 %fusion.27 = bf16[20,256,128]{1,2,0:T(8,128)(2,1)} fusion(bf16[256,20,128]{0,2,1:T(8,128)(2,1)} %bitcast.55, f32[20,256,256]{1,2,0:T(8,128)} %fusion.45, f32[20,256,256]{1,2,0:T(8,128)} %get-tuple-element.23, f32[20,256]{1,0:T(8,128)S(1)} %get-tuple-element.22), kind=kOutput, calls=%fused_computation.30 | convolution fusion | flops 345380096 | bytes 13127680 | tf_op jit(solution)/shard_map/hqk,khd->qhd/dot_general | solution.py:85
  241.4 0.0 copy-start.5
  241.4 2.5 copy.56
  243.9 0.0 copy-done.5
  243.9 10.1 %fusion.30 = bf16[20,256,128]{1,2,0:T(8,128)(2,1)} fusion(bf16[256,20,128]{0,2,1:T(8,128)(2,1)S(1)} %bitcast.53, f32[20,256,256]{1,2,0:T(8,128)} %fusion.45, f32[20,256,256]{1,2,0:T(8,128)} %get-tuple-element.23, f32[20,256]{1,0:T(8,128)S(1)} %get-tuple-element.22), kind=kOutput, calls=%fused_computation.31 | convolution fusion | flops 345380096 | bytes 13127680 | tf_op jit(solution)/shard_map/hqk,qhd->khd/dot_general | solution.py:90
  254.0 2.4 copy.57
  256.4 104.1 %reduce-scatter.2.cloned.1.call-done = bf16[160,2560]{1,0:T(8,128)(2,1)} async-done(((bf16[2560,2560]{1,0:T(8,128)(2,1)}), bf16[160,2560]{1,0:T(8,128)(2,1)}) %reduce-scatter.2.cloned.1.call-update) | async-done | bytes 819216 | tf_op jit(solution)/shard_map/reduce_scatter | solution.py:67
  360.5 0.0 all-reduce.2.cloned.1.call-update
  360.5 3.5 convolution_convert_fusion.2
  364.0 1.6 copy.58
  365.6 63.0 %all-reduce.2.cloned.1.call-done = bf16[1,160,2560]{2,1,0:T(8,128)(2,1)} async-done(((bf16[1,160,2560]{2,1,0:T(8,128)(2,1)}), bf16[1,160,2560]{2,1,0:T(8,128)(2,1)}) %all-reduce.2.cloned.1.call-update) | async-done | bytes 819216 | tf_op jit(solution)/shard_map/psum | solution.py:70
  428.6 2.5 broadcast_in_dim.54
  (3 shorter events, 0.0 us)
Async XLA Ops:
  7.2 2.4 copy-start.3
  7.2 152.9 %all-gather.3.cloned.1.call-start = ((), (), s32[]{:S(2)}) async-start(), calls=%async_computation.3 | async-start | bytes 13926400 | tf_op jit(solution)/shard_map/all_gather | solution.py:23
  7.9 352.6 %reduce-scatter.2.cloned.1.call-start = ((), (), s32[]{:S(2)}) async-start(), calls=%async_computation.1 | async-start | bytes 13926400 | tf_op jit(solution)/shard_map/reduce_scatter | solution.py:67
  9.6 11.0 %copy-start = (bf16[1,1,256,2560]{2,3,1,0:T(8,128)(2,1)}, bf16[1,1,256,2560]{2,3,1,0:T(8,128)(2,1)S(1)}, u32[]{:S(2)}) copy-start(bf16[1,1,256,2560]{2,3,1,0:T(8,128)(2,1)S(1)} %copy.48) | copy-start | bytes 3932164
  9.6 4.0 copy-start.9
  9.6 4.6 %copy-start.6 = (f32[1,2560]{1,0:T(1,128)S(1)}, f32[1,2560]{1,0:T(1,128)}, u32[]{:S(2)}) copy-start(f32[1,2560]{1,0:T(1,128)} %param.17) | copy-start | bytes 30724
  11.1 3.9 copy-start.4
  169.2 5.1 %copy-start.7 = (f32[1024]{0:T(1024)S(1)}, f32[1024]{0:T(1024)}, u32[]{:S(2)}) copy-start(f32[1024]{0:T(1024)} %param.15) | copy-start | bytes 12292
  169.3 5.1 %copy-start.8 = (s32[1,256]{1,0:T(1,128)S(1)}, s32[1,256]{1,0:T(1,128)}, u32[]{:S(2)}) copy-start(s32[1,256]{1,0:T(1,128)} %param.13) | copy-start | bytes 3076
  170.6 32.2 %collective-permute-start = (bf16[256,2560]{1,0:T(8,128)(2,1)}, bf16[256,2560]{1,0:T(8,128)(2,1)}, u32[]{:S(2)}, u32[]{:S(2)}) collective-permute-start(bf16[256,2560]{1,0:T(8,128)(2,1)} %multiply_convert_fusion.2), channel_id=1, source_target_pairs={{0,128},{128,0},{1,129},{129,1},{2,130},{130,2},{3,131},{131,3},{4... | collective-permute-start | bytes 3932168 | tf_op jit(solution)/shard_map/ppermute | solution.py:10
  174.3 30.9 %copy-start.2 = (bf16[20,256,128]{1,2,0:T(8,128)(2,1)S(1)}, bf16[20,256,128]{1,2,0:T(8,128)(2,1)}, u32[]{:S(2)}) copy-start(bf16[20,256,128]{1,2,0:T(8,128)(2,1)} %convolution_convert_fusion.1) | copy-start | bytes 3932164
  213.9 214.7 %all-reduce.2.cloned.1.call-start = ((), (), s32[]{:S(2)}) async-start(), calls=%async_computation.2 | async-start | bytes 1638400 | tf_op jit(solution)/shard_map/psum | solution.py:70
  226.1 1.7 copy-start.1
  241.4 2.5 copy-start.5
Sparse Core Ops, SparseCore 0:
  9.8 150.2 all-gather.2
  214.0 146.4 reduce-scatter.1
  362.9 65.7 all-reduce.1
where the time goes:
time: 439 us
  waiting for transfers between devices  331 us (75%)
  matrix products  64.6 us (15%)
  between operations  16.3 us (4%)
  local copies, waits for them, and re-layouts  14.4 us (3%)
  other arithmetic  9.98 us (2%)
    all_gather x1, waiting for transfers between devices, body(): full_weight = lax.all_gather(w_out[0], 'fsdp', axis=0, tiled=True)  135 us
    reduce_scatter x1, waiting for transfers between devices, body(): lax.psum_scatter(partial_term, 'fsdp', scatter_dimension=0, tiled=True)  104 us
    psum x1, waiting for transfers between devices, body(): d_wo = lax.psum(row_sum.astype(jnp.bfloat16), 'dp').astype(jnp.float32)  63 us
    ppermute x1, waiting for transfers between devices, partner_2(): lax.ppermute(value, axis, [(i, i ^ 1 << bit) for i in range(lax.axis_size...  27.4 us
    unnamed x26, local copies, waits for them, and re-layouts  12.1 us
    dot_general x1, matrix products, body(): jnp.einsum('hqk,khd->qhd', ds, key_heads, preferred_element_type=jnp.floa...  10.4 us
    dot_general x1, matrix products, body(): jnp.einsum('hqk,qhd->khd', ds, query_heads, preferred_element_type=jnp.fl...  10.1 us
    dot_general x1, matrix products, body(): lax.dot_general(d_hidden, full_weight, (((1,), (1,)), ((), ())), preferre...  10 us
  transfers between devices with their start and end apart: 4, of which 4 were waited for; matrix products, arithmetic and copies ran while one was open for 15% of the time, Pallas kernels for 0%

commit v1 on v0

--- a/solution.py
+++ b/solution.py
@@ -4,6 +4,11 @@
 from jax.sharding import PartitionSpec as P
 
 DH = 128
+
+
+def gather_and_add(shard, mesh_axis):
+    parts = lax.all_gather(shard, mesh_axis)
+    return jnp.sum(parts, axis=0)
 
 
 def partner_2(value, axis, bit):
@@ -67,7 +72,7 @@
     row_sum = lax.psum_scatter(partial_term, "fsdp", scatter_dimension=0, tiled=True).astype(
         jnp.float32
     )
-    d_wo = lax.psum(row_sum.astype(jnp.bfloat16), "dp").astype(jnp.float32)
+    d_wo = gather_and_add(row_sum.astype(jnp.bfloat16), "dp").astype(jnp.float32)
     d_attn_arranged = lax.dot_general(
         d_hidden, full_weight, (((1,), (1,)), ((), ())), preferred_element_type=jnp.float32
     )

time: 439 us -> 424 us (0.966)
  waiting for transfers between devices: 331 us -> 310 us
    psum x1 -> x0, waiting for transfers between devices: 63 us -> none  [body(): d_wo = lax.psum(row_sum.astype(jnp.bfloat16), 'dp').astype(jnp.float32)]
    reduce_scatter x1, waiting for transfers between devices: 104 us -> 146 us  [body(): lax.psum_scatter(partial_term, 'fsdp', scatter_dimension=0, tiled=True)]
  transfers between devices with their start and end apart: 4 -> 4, of which waited for: 4 -> 3; matrix products, arithmetic and copies ran while one was open for 15% -> 15% of each run, Pallas kernels for 0% -> 0%
where the time goes in v1:
time: 424 us; the launch traced here: 422 us
  waiting for transfers between devices  310 us (73%)
  matrix products  64.9 us (15%)
  between operations  16.3 us (4%)
  local copies, waits for them, and re-layouts  14.7 us (3%)
  other arithmetic  13 us (3%)
    reduce_scatter x1, waiting for transfers between devices, body(): lax.psum_scatter(partial_term, 'fsdp', scatter_dimension=0, tiled=True)  146 us
    all_gather x1, waiting for transfers between devices, body(): full_weight = lax.all_gather(w_out[0], 'fsdp', axis=0, tiled=True)  135 us
    ppermute x1, waiting for transfers between devices, partner_2(): lax.ppermute(value, axis, [(i, i ^ 1 << bit) for i in range(lax.axis_size...  27.4 us
    unnamed x26, local copies, waits for them, and re-layouts  12.3 us
    dot_general x1, matrix products, body(): jnp.einsum('hqk,khd->qhd', ds, key_heads, preferred_element_type=jnp.floa...  10.4 us
    dot_general x1, matrix products, body(): jnp.einsum('hqk,qhd->khd', ds, query_heads, preferred_element_type=jnp.fl...  10.3 us
    dot_general x1, matrix products, body(): lax.dot_general(d_hidden, full_weight, (((1,), (1,)), ((), ())), preferre...  10 us
    dot_general x1, matrix products, body(): jnp.dot(arrange(attn), full_weight, preferred_element_type=jnp.float32)  9.16 us
  transfers between devices with their start and end apart: 4, of which 3 were waited for; matrix products, arithmetic and copies ran while one was open for 15% of the time, Pallas kernels for 0%

profile of v1, /device:TPU:8, one launch (start us, length us, event | category | flops | bytes accessed | tf_op | source)
XLA Modules:
  0.0 421.6 jit_solution(4373585531279610610)
XLA Ops:
  7.2 0.0 copy-start.3
  7.2 0.0 all-gather.5.cloned.1.call-start
  7.2 0.7 all-gather.5.cloned.1.call-update
  7.9 0.0 reduce-scatter.2.cloned.1.call-start
  8.0 1.6 copy.48
  9.6 0.0 copy-start
  9.6 0.0 copy-done.3
  9.6 0.0 copy-start.9
  9.6 0.0 copy-start.6
  9.6 1.4 copy.44
  11.1 0.0 copy-start.4
  11.1 2.5 copy.45
  13.6 0.0 copy-done.9
  13.6 0.6 dynamic_slice.3
  14.2 0.0 copy-done.6
  14.2 0.7 iota_compare_fusion.2
  14.9 0.1 fusion.35
  15.0 0.0 copy-done.4
  15.0 5.6 %fusion.44 = (f32[20,256]{1,0:T(8,128)S(1)}, f32[20,256,256]{1,2,0:T(8,128)}) fusion(pred[256,256]{0,1:T(8,128)(4,1)S(1)} %fusion.35, bf16[256,20,128]{0,2,1:T(8,128)(2,1)S(1)} %bitcast.56, bf16[256,20,128]{0,2,1:T(8,128)(2,1)} %bitcast.58), kind=kOutput, calls=%fused_computation.53 | convolution fusion | flops 340787456 | bytes 7950336 | tf_op jit(solution)/shard_map/sub | solution.py:43
  20.6 0.0 copy-done
  20.6 4.1 convolution_convert_fusion.1
  24.7 135.4 %all-gather.5.cloned.1.call-done = bf16[1,2560,2560]{2,1,0:T(8,128)(2,1)} async-done(((bf16[1,160,2560]{2,1,0:T(8,128)(2,1)}), bf16[1,2560,2560]{2,1,0:T(8,128)(2,1)}) %all-gather.5.cloned.1.call-update) | async-done | bytes 13107216 | tf_op jit(solution)/shard_map/all_gather | solution.py:28
  160.1 9.2 %multiply_reduce_fusion.3 = (f32[256]{0:T(256)S(1)}, f32[256,2560]{1,0:T(8,128)S(1)}) fusion(bf16[256,2560]{0,1:T(8,128)(2,1)} %bitcast.54, bf16[1,2560,2560]{2,1,0:T(8,128)(2,1)} %all-gather.5.cloned.1.call-done, bf16[1,1,256,2560]{3,2,1,0:T(8,128)(2,1)} %param.12), kind=kOutput, calls=%fused_computation.22 | convolution fusion | flops 3358064384 | bytes 18351104 | tf_op jit(solution)/shard_map/dot_general | solution.py:50
  169.2 0.0 copy-start.7
  169.3 0.0 copy-start.8
  169.3 1.3 multiply_convert_fusion.2
  170.6 2.4 collective-permute-start
  173.0 0.7 reduce_sum.89
  174.3 0.0 copy-start.2
  174.3 0.0 copy-done.7
  174.3 0.0 copy-done.8
  174.3 0.2 select_reduce_fusion
  174.6 0.8 select_multiply_fusion
  175.4 27.4 %collective-permute-done = bf16[256,2560]{1,0:T(8,128)(2,1)} collective-permute-done((bf16[256,2560]{1,0:T(8,128)(2,1)}, bf16[256,2560]{1,0:T(8,128)(2,1)}, u32[]{:S(2)}, u32[]{:S(2)}) %collective-permute-start) | collective-permute-done | bytes 1310752 | tf_op jit(solution)/shard_map/ppermute | solution.py:15
  202.8 2.4 multiply_reduce_fusion.1
  205.3 0.0 copy-done.2
  205.3 8.6 %convolution_convert_fusion = bf16[2560,2560]{1,0:T(8,128)(2,1)} fusion(bf16[256,2560]{0,1:T(8,128)(2,1)S(1)} %bitcast.55, f32[256,2560]{1,0:T(8,128)S(1)} %get-tuple-element.25, bf16[256,2560]{1,0:T(8,128)(2,1)} %collective-permute-done, f32[256]{0:T(256)S(1)} %broadcast_multiply_fusion, f32[]{:T(128)S(6)} %mul.91, f32[256]{0:T(256)S(1)} %select_multiply_fusion, ...), kind=kOutput, calls=%fused_computation.2 | convolution fusion | flops 3369205760 | bytes 18363396 | tf_op jit(solution)/shard_map/dot_general | solution.py:69
  213.9 0.0 reduce-scatter.2.cloned.1.call-update
  213.9 0.2 all-gather.7.cloned.1.call-start
  214.1 146.4 %reduce-scatter.2.cloned.1.call-done = bf16[160,2560]{1,0:T(8,128)(2,1)} async-done(((bf16[2560,2560]{1,0:T(8,128)(2,1)}), bf16[160,2560]{1,0:T(8,128)(2,1)}) %reduce-scatter.2.cloned.1.call-update) | async-done | bytes 819216 | tf_op jit(solution)/shard_map/reduce_scatter | solution.py:72
  360.5 0.0 all-gather.7.cloned.1.call-update
  360.5 1.2 multiply_reduce_fusion.4
  362.4 10.0 %fusion.11 = bf16[256,2560]{1,0:T(8,128)(2,1)} fusion(bf16[1,2560,2560]{2,1,0:T(8,128)(2,1)} %all-gather.5.cloned.1.call-done, f32[256,2560]{1,0:T(8,128)S(1)} %get-tuple-element.25, bf16[256,2560]{1,0:T(8,128)(2,1)} %collective-permute-done, f32[256]{0:T(256)S(1)} %broadcast_multiply_fusion, f32[]{:T(128)S(6)} %mul.91, f32[256]{0:T(256)S(1)} %select_multiply_fusion, ...), kind=kOutput, calls=%fused_computation.14 | convolution fusion | flops 3363307520 | bytes 18363396 | tf_op jit(solution)/shard_map/dot_general | solution.py:76
  372.5 0.0 copy-start.1
  372.5 1.8 copy.50
  374.2 0.2 copy-done.1
  374.4 3.2 fusion.45
  377.6 10.4 %fusion.27 = bf16[20,256,128]{1,2,0:T(8,128)(2,1)} fusion(bf16[256,20,128]{0,2,1:T(8,128)(2,1)} %bitcast.59, f32[20,256,256]{1,2,0:T(8,128)} %fusion.45, f32[20,256,256]{1,2,0:T(8,128)} %get-tuple-element.23, f32[20,256]{1,0:T(8,128)S(1)} %get-tuple-element.22), kind=kOutput, calls=%fused_computation.30 | convolution fusion | flops 345380096 | bytes 13127680 | tf_op jit(solution)/shard_map/hqk,khd->qhd/dot_general | solution.py:90
  388.0 0.0 copy-start.5
  388.0 2.5 copy.56
  390.5 0.0 copy-done.5
  390.5 10.3 %fusion.30 = bf16[20,256,128]{1,2,0:T(8,128)(2,1)} fusion(bf16[256,20,128]{0,2,1:T(8,128)(2,1)S(1)} %bitcast.57, f32[20,256,256]{1,2,0:T(8,128)} %fusion.45, f32[20,256,256]{1,2,0:T(8,128)} %get-tuple-element.23, f32[20,256]{1,0:T(8,128)S(1)} %get-tuple-element.22), kind=kOutput, calls=%fused_computation.31 | convolution fusion | flops 345380096 | bytes 13127680 | tf_op jit(solution)/shard_map/hqk,qhd->khd/dot_general | solution.py:95
  400.8 2.4 copy.57
  403.3 3.6 convolution_convert_fusion.2
  406.8 1.6 copy.58
  408.4 0.0 all-gather.7.cloned.1.call-done
  408.4 4.2 reduce_sum.92
  412.6 1.3 bitcast_convert_fusion
  (3 shorter events, 0.0 us)
Async XLA Ops:
  7.2 2.4 copy-start.3
  7.2 152.9 %all-gather.5.cloned.1.call-start = ((), (), s32[]{:S(2)}) async-start(), calls=%async_computation.2 | async-start | bytes 13926400 | tf_op jit(solution)/shard_map/all_gather | solution.py:28
  7.9 352.6 %reduce-scatter.2.cloned.1.call-start = ((), (), s32[]{:S(2)}) async-start(), calls=%async_computation.1 | async-start | bytes 13926400 | tf_op jit(solution)/shard_map/reduce_scatter | solution.py:72
  9.6 11.0 %copy-start = (bf16[1,1,256,2560]{2,3,1,0:T(8,128)(2,1)}, bf16[1,1,256,2560]{2,3,1,0:T(8,128)(2,1)S(1)}, u32[]{:S(2)}) copy-start(bf16[1,1,256,2560]{2,3,1,0:T(8,128)(2,1)S(1)} %copy.48) | copy-start | bytes 3932164
  9.6 4.0 copy-start.9
  9.6 4.6 %copy-start.6 = (f32[1,2560]{1,0:T(1,128)S(1)}, f32[1,2560]{1,0:T(1,128)}, u32[]{:S(2)}) copy-start(f32[1,2560]{1,0:T(1,128)} %param.17) | copy-start | bytes 30724
  11.1 3.9 copy-start.4
  169.2 5.1 %copy-start.7 = (f32[1024]{0:T(1024)S(1)}, f32[1024]{0:T(1024)}, u32[]{:S(2)}) copy-start(f32[1024]{0:T(1024)} %param.15) | copy-start | bytes 12292
  169.3 5.1 %copy-start.8 = (s32[1,256]{1,0:T(1,128)S(1)}, s32[1,256]{1,0:T(1,128)}, u32[]{:S(2)}) copy-start(s32[1,256]{1,0:T(1,128)} %param.13) | copy-start | bytes 3076
  170.6 32.2 %collective-permute-start = (bf16[256,2560]{1,0:T(8,128)(2,1)}, bf16[256,2560]{1,0:T(8,128)(2,1)}, u32[]{:S(2)}, u32[]{:S(2)}) collective-permute-start(bf16[256,2560]{1,0:T(8,128)(2,1)} %multiply_convert_fusion.2), channel_id=1, source_target_pairs={{0,128},{128,0},{1,129},{129,1},{2,130},{130,2},{3,131},{131,3},{4... | collective-permute-start | bytes 3932168 | tf_op jit(solution)/shard_map/ppermute | solution.py:15
  174.3 30.9 %copy-start.2 = (bf16[20,256,128]{1,2,0:T(8,128)(2,1)S(1)}, bf16[20,256,128]{1,2,0:T(8,128)(2,1)}, u32[]{:S(2)}) copy-start(bf16[20,256,128]{1,2,0:T(8,128)(2,1)} %convolution_convert_fusion.1) | copy-start | bytes 3932164
  213.9 194.5 %all-gather.7.cloned.1.call-start = ((), (), s32[]{:S(2)}) async-start(), calls=%async_computation.3 | async-start | bytes 7372800 | tf_op jit(solution)/shard_map/all_gather | solution.py:10
  372.5 2.0 copy-start.1
  388.0 2.5 copy-start.5
Sparse Core Ops, SparseCore 0:
  9.8 150.2 all-gather.4
  214.0 146.4 reduce-scatter.1
  362.3 43.1 all-gather.6
